TPU v7x, 32 devices: a whole 2x2x4 slice. The times are simulated.
32 devices in a mesh: section: 4 (over y, x), expert: 4 (over z), dp: 2 (over core).
Axes of the slice: x: 2, y: 2, z: 4, core: 2. Of those that a mesh axis runs over, the one named last changes fastest.
Arguments:
- activations: bfloat16 [4, 1024, 4096], P('section', ('dp', 'expert')), parts along dimension 1, may hold values from -6 to 6
- routes: int32 [2, 4, 1024, 2], P(None, 'section', ('dp', 'expert')), parts along dimension 2, may hold values from 0 to 3, all different within a row; in each aligned block of 128 rows (0 to 127, 128 to 255, ..., all dimensions but the last counted through in order) at most 72 rows name the same one
- combine: float32 [2, 4, 1024, 2], P(None, 'section', ('dp', 'expert')), parts along dimension 2, may hold values from 0.2 to 1
- norm_gain: float32 [4, 4096], P('section'), may hold values from 0.5 to 2
- up_weight: bfloat16 [4, 4, 4096, 768], P('section', 'expert'), may hold values from -0.09375 to 0.09375
- down_weight: bfloat16 [4, 4, 768, 4096], P('section', 'expert'), may hold values from -0.21875 to 0.21875
Outputs:
- carried: bfloat16 [4, 1024, 4096], P('section', ('dp', 'expert')), parts along dimension 1
There are 2 independent parts, one for each index of `dp`. A program takes and returns all parts, laid end to end along the dimension named above; an argument that names none is the same for every part. Nothing has to cross between parts.
Inputs may be any that keep to these rules, and one draw needn't show every extreme that they name: `routes`: in each aligned block of 128 rows (the rows of one device) no expert is named by more than 72 pairs; the ids of one row differ.
All inputs are finite; a program needn't handle non-finite values.
Results may differ from a plain program's by a relative error of at most 0.007.
Values may be sent and summed in bfloat16 or wider, within the bound.
A program may use at most 128 MiB of HBM per device.

v0:
```python
import jax
import jax.numpy as jnp
from jax import lax
from jax.sharding import PartitionSpec as P

STOPS = 2


def from_behind(value, axis, steps):
    count = lax.axis_size(axis)
    pairs = [(source, (source + steps) % count) for source in range(count)]
    return lax.ppermute(value, axis, pairs)


def slot_of(expert_ids, experts):
    flattened = expert_ids.reshape(-1)
    onehot = (flattened[:, None] == jnp.arange(experts, dtype=jnp.int32)[None, :]).astype(jnp.int32)
    before = jnp.cumsum(onehot, axis=0) - onehot
    return jnp.sum(before * onehot, axis=1).reshape(expert_ids.shape)


def body(activations, routes, combine, norm_gain, up_weight, down_weight):
    state = activations[0]
    gain_row = norm_gain[0]
    up_proj = up_weight[0, 0]
    down_proj = down_weight[0, 0]
    experts = lax.axis_size("expert")
    tok_rows = state.shape[0]
    width = state.shape[1]
    chosen = routes.shape[3]
    capacity = tok_rows * chosen // experts * 9 // 8
    for visit in range(STOPS):
        expert_ids = routes[visit, 0]
        weights_now = combine[visit, 0]
        wide_state = state.astype(jnp.float32)
        normed = (
            wide_state
            * lax.rsqrt(jnp.mean(wide_state * wide_state, axis=-1, keepdims=True) + 1e-06)
            * gain_row
        ).astype(jnp.bfloat16)
        slots = slot_of(expert_ids, experts)
        spread = jnp.broadcast_to(normed[:, None, :], (tok_rows, chosen, width))
        outbox = (
            jnp.zeros((experts, capacity, width), jnp.bfloat16).at[expert_ids, slots].set(spread)
        )
        arrived = lax.all_to_all(outbox, "expert", split_axis=0, concat_axis=0, tiled=True)
        hidden = jax.nn.silu(
            jnp.dot(arrived.reshape(-1, width), up_proj, preferred_element_type=jnp.float32)
        ).astype(jnp.bfloat16)
        served = (
            jnp.dot(hidden, down_proj, preferred_element_type=jnp.float32)
            .astype(jnp.bfloat16)
            .reshape(arrived.shape)
        )
        returned = lax.all_to_all(served, "expert", split_axis=0, concat_axis=0, tiled=True)
        picked = returned[expert_ids, slots].astype(jnp.float32)
        mixed = (wide_state + jnp.sum(picked * weights_now[..., None], axis=1)).astype(jnp.bfloat16)
        state = from_behind(mixed, "section", 1)
    return state[None]


def solution(mesh):
    placed = (
        P("section", ("dp", "expert"), None),
        P(None, "section", ("dp", "expert"), None),
        P(None, "section", ("dp", "expert"), None),
        P("section", None),
        P("section", "expert", None, None),
        P("section", "expert", None, None),
    )
    return jax.shard_map(
        body,
        mesh=mesh,
        in_specs=placed,
        out_specs=P("section", ("dp", "expert"), None),
        check_vma=False,
    )
```

profile of v0, /device:TPU:0, one launch (start us, length us, event | category | flops | bytes accessed | tf_op | source)
XLA Modules:
  0.0 464.2 jit_solution(4136053193010869689)
XLA Ops:
  0.0 0.0 copy-start
  0.0 0.8 fusion.46
  0.8 0.1 copy.21
  0.9 0.1 eq.54
  1.0 0.1 eq.50
  1.2 1.5 fusion.18
  2.7 1.2 reduce-window.14
  4.0 0.1 slice.40
  4.0 0.1 copy.14
  4.2 0.1 copy.15
  4.3 0.1 add_bitcast_fusion.1
  4.4 0.1 reshape.217
  4.6 0.1 reshape.237
  4.7 0.0 copy-done
  4.7 1.0 fusion.20
  5.8 2.1 broadcast_in_dim.6
  7.9 2.2 reshape.239
  10.1 0.3 broadcast.141.clone
  10.4 48.8 %scatter_fusion = bf16[4,72,4096]{2,1,0:T(8,128)(2,1)S(1)} fusion(bf16[4,72,4096]{2,1,0:T(8,128)(2,1)S(1)} %broadcast.141.clone, s32[256]{0:T(256)S(1)} %reshape.237, bf16[256,4096]{1,0:T(8,128)(2,1)} %reshape.239), kind=kCustom, calls=%fused_computation.2 | custom fusion | bytes 6293504 | tf_op jit(solution)/shard_map/scatter | solution.py:44
  59.2 60.1 %all_to_all.20 = bf16[4,72,4096]{2,1,0:T(8,128)(2,1)} all-to-all(bf16[4,72,4096]{2,1,0:T(8,128)(2,1)S(1)} %scatter_fusion), channel_id=1, replica_groups=mesh['section'=4,'expert'=4,'dp'=2] {'expert'}, dimensions={0} | all-to-all | bytes 4718592 | tf_op jit(solution)/shard_map/all_to_all | solution.py:46
  119.2 11.8 %fusion.8 = bf16[288,4096]{1,0:T(8,128)(2,1)} fusion(bf16[1,1,768,4096]{3,2,1,0:T(8,128)(2,1)} %param.11, bf16[288,4096]{1,0:T(8,128)(2,1)} %bitcast.113, bf16[1,1,4096,768]{3,2,1,0:T(8,128)(2,1)} %param.10), kind=kOutput, calls=%fused_computation.12 | convolution fusion | flops 3626164224 | bytes 17301504 | tf_op jit(solution)/shard_map/dot_general | solution.py:51
  131.0 0.0 copy-start.2
  131.0 4.0 all-to-all-start.1
  135.0 0.1 reshape.225
  135.1 0.0 copy-done.2
  135.2 0.1 copy.16
  135.3 52.7 %all-to-all-done.1 = bf16[4,72,4096]{2,1,0:T(8,128)(2,1)S(1)} async-done(((bf16[4,72,4096]{2,1,0:T(8,128)(2,1)}), bf16[4,72,4096]{2,1,0:T(8,128)(2,1)S(1)}, u32[]{:S(2)}, u32[]{:S(2)}) %all-to-all-start.1) | async-done | bytes 2359328 | tf_op jit(solution)/shard_map/all_to_all | solution.py:55
  188.0 8.5 %gather_fusion = bf16[256,4096]{1,0:T(8,128)(2,1)} fusion(bf16[4,72,4096]{2,1,0:T(8,128)(2,1)S(1)} %all-to-all-done.1, s32[256]{0:T(256)S(1)} %reshape.225), kind=kCustom, calls=%fused_computation | custom fusion | bytes 4196352 | tf_op jit(solution)/shard_map/gather | solution.py:56
  196.5 5.8 %reshape.249 = f32[128,2,4096]{2,1,0:T(2,128)} reshape(bf16[256,4096]{1,0:T(8,128)(2,1)} %gather_fusion) | data formatting | bytes 6291456 | tf_op jit(solution)/shard_map/convert_element_type | solution.py:56
  202.3 8.8 %multiply_reduce_fusion.1 = f32[128,4096]{1,0:T(8,128)S(1)} fusion(f32[128,2,4096]{2,1,0:T(2,128)} %reshape.249, f32[128,2]{1,0:T(8,128)S(1)} %copy.16), kind=kLoop, calls=%fused_computation.15 | loop fusion | flops 1572864 | bytes 6292480 | tf_op jit(solution)/shard_map/reduce_sum | solution.py:57
  211.1 0.0 copy-start.1
  211.1 0.2 fusion.21
  211.4 1.5 collective-permute-start
  212.9 0.1 copy.22
  213.0 0.1 eq.62
  213.1 0.1 eq.58
  213.3 1.2 reduce-window.16
  214.5 0.1 slice.41
  214.6 0.1 copy.18
  214.8 0.1 copy.19
  214.8 0.1 add_bitcast_fusion
  214.9 0.1 reshape.221
  215.1 0.1 reshape.243
  215.3 21.2 %collective-permute-done = bf16[128,4096]{1,0:T(8,128)(2,1)S(1)} collective-permute-done((bf16[128,4096]{1,0:T(8,128)(2,1)S(1)}, bf16[128,4096]{1,0:T(8,128)(2,1)S(1)}, u32[]{:S(2)}, u32[]{:S(2)}) %collective-permute-start) | collective-permute-done | bytes 1048608 | tf_op jit(solution)/shard_map/ppermute | solution.py:12
  236.5 0.3 fusion.14
  236.8 0.0 copy-done.1
  236.8 0.3 fusion.16
  237.1 2.1 broadcast_in_dim.7
  239.2 2.2 reshape.245
  241.5 0.3 broadcast.141
  241.7 48.8 %scatter_fusion.1 = bf16[4,72,4096]{2,1,0:T(8,128)(2,1)S(1)} fusion(bf16[4,72,4096]{2,1,0:T(8,128)(2,1)S(1)} %broadcast.141, s32[256]{0:T(256)S(1)} %reshape.243, bf16[256,4096]{1,0:T(8,128)(2,1)} %reshape.245), kind=kCustom, calls=%fused_computation.3 | custom fusion | bytes 6293504 | tf_op jit(solution)/shard_map/scatter | solution.py:44
  290.6 55.9 %all_to_all.21 = bf16[4,72,4096]{2,1,0:T(8,128)(2,1)} all-to-all(bf16[4,72,4096]{2,1,0:T(8,128)(2,1)S(1)} %scatter_fusion.1), channel_id=1, replica_groups=mesh['section'=4,'expert'=4,'dp'=2] {'expert'}, dimensions={0} | all-to-all | bytes 4718592 | tf_op jit(solution)/shard_map/all_to_all | solution.py:46
  346.5 11.8 %fusion.11 = bf16[288,4096]{1,0:T(8,128)(2,1)} fusion(bf16[1,1,768,4096]{3,2,1,0:T(8,128)(2,1)} %param.11, bf16[288,4096]{1,0:T(8,128)(2,1)} %bitcast.114, bf16[1,1,4096,768]{3,2,1,0:T(8,128)(2,1)} %param.10), kind=kOutput, calls=%fused_computation.13 | convolution fusion | flops 3626164224 | bytes 17301504 | tf_op jit(solution)/shard_map/dot_general | solution.py:51
  358.3 3.6 all-to-all-start.3
  361.9 0.1 copy.20
  362.0 0.1 reshape.231
  362.2 52.5 %all-to-all-done.3 = bf16[4,72,4096]{2,1,0:T(8,128)(2,1)S(1)} async-done(((bf16[4,72,4096]{2,1,0:T(8,128)(2,1)}), bf16[4,72,4096]{2,1,0:T(8,128)(2,1)S(1)}, u32[]{:S(2)}, u32[]{:S(2)}) %all-to-all-start.3) | async-done | bytes 2359328 | tf_op jit(solution)/shard_map/all_to_all | solution.py:55
  414.6 8.5 %gather_fusion.1 = bf16[256,4096]{1,0:T(8,128)(2,1)} fusion(bf16[4,72,4096]{2,1,0:T(8,128)(2,1)S(1)} %all-to-all-done.3, s32[256]{0:T(256)S(1)} %reshape.231), kind=kCustom, calls=%fused_computation.1 | custom fusion | bytes 4196352 | tf_op jit(solution)/shard_map/gather | solution.py:56
  423.2 5.6 %reshape.250 = f32[128,2,4096]{2,1,0:T(2,128)} reshape(bf16[256,4096]{1,0:T(8,128)(2,1)} %gather_fusion.1) | data formatting | bytes 6291456 | tf_op jit(solution)/shard_map/convert_element_type | solution.py:56
  428.8 8.8 %multiply_reduce_fusion = f32[128,4096]{1,0:T(8,128)S(1)} fusion(f32[128,2,4096]{2,1,0:T(2,128)} %reshape.250, f32[128,2]{1,0:T(8,128)S(1)} %copy.20), kind=kLoop, calls=%fused_computation.14 | loop fusion | flops 1572864 | bytes 6292480 | tf_op jit(solution)/shard_map/reduce_sum | solution.py:57
  437.6 0.3 fusion.17
  437.8 0.6 collective-permute-start.1
  438.5 24.5 %collective-permute-done.1 = bf16[128,4096]{1,0:T(8,128)(2,1)S(1)} collective-permute-done((bf16[128,4096]{1,0:T(8,128)(2,1)S(1)}, bf16[128,4096]{1,0:T(8,128)(2,1)S(1)}, u32[]{:S(2)}, u32[]{:S(2)}) %collective-permute-start.1) | collective-permute-done | bytes 1048608 | tf_op jit(solution)/shard_map/ppermute | solution.py:12
  463.0 1.0 copy.30
  (13 shorter events, 0.2 us)
Async XLA Ops:
  0.0 4.7 %copy-start = (bf16[1,128,4096]{2,1,0:T(8,128)(2,1)S(1)}, bf16[1,128,4096]{2,1,0:T(8,128)(2,1)}, u32[]{:S(2)}) copy-start(bf16[1,128,4096]{2,1,0:T(8,128)(2,1)} %param.6) | copy-start | bytes 3145732
  131.0 4.1 copy-start.2
  131.0 56.9 %all-to-all-start.1 = ((bf16[4,72,4096]{2,1,0:T(8,128)(2,1)}), bf16[4,72,4096]{2,1,0:T(8,128)(2,1)S(1)}, u32[]{:S(2)}, u32[]{:S(2)}) async-start(bf16[4,72,4096]{2,1,0:T(8,128)(2,1)} %bitcast.111), calls=%async_computation.1 | async-start | bytes 4718592 | tf_op jit(solution)/shard_map/all_to_all | solution.py:55
  211.1 25.7 %copy-start.1 = (f32[1,4096]{1,0:T(1,128)S(1)}, f32[1,4096]{1,0:T(1,128)}, u32[]{:S(2)}) copy-start(f32[1,4096]{1,0:T(1,128)} %param.9) | copy-start | bytes 49156
  211.4 25.1 %collective-permute-start = (bf16[128,4096]{1,0:T(8,128)(2,1)S(1)}, bf16[128,4096]{1,0:T(8,128)(2,1)S(1)}, u32[]{:S(2)}, u32[]{:S(2)}) collective-permute-start(bf16[128,4096]{1,0:T(8,128)(2,1)S(1)} %fusion.21), channel_id=1, source_target_pairs={{0,8},{8,16},{16,24},{24,0},{1,9},{9,17},{17,25},{25,1},{2,10},{10... | collective-permute-start | bytes 3145736 | tf_op jit(solution)/shard_map/ppermute | solution.py:12
  358.3 56.4 %all-to-all-start.3 = ((bf16[4,72,4096]{2,1,0:T(8,128)(2,1)}), bf16[4,72,4096]{2,1,0:T(8,128)(2,1)S(1)}, u32[]{:S(2)}, u32[]{:S(2)}) async-start(bf16[4,72,4096]{2,1,0:T(8,128)(2,1)} %bitcast.112), calls=%async_computation.3 | async-start | bytes 4718592 | tf_op jit(solution)/shard_map/all_to_all | solution.py:55
  437.8 25.1 %collective-permute-start.1 = (bf16[128,4096]{1,0:T(8,128)(2,1)S(1)}, bf16[128,4096]{1,0:T(8,128)(2,1)S(1)}, u32[]{:S(2)}, u32[]{:S(2)}) collective-permute-start(bf16[128,4096]{1,0:T(8,128)(2,1)S(1)} %fusion.17), channel_id=1, source_target_pairs={{0,8},{8,16},{16,24},{24,0},{1,9},{9,17},{17,25},{25,1},{2,10},{10... | collective-permute-start | bytes 3145736 | tf_op jit(solution)/shard_map/ppermute | solution.py:12
where the time goes:
time: 472 us; the launch traced here: 464 us
  waiting for transfers between devices  151 us (32%)
  local copies, waits for them, and re-layouts  139 us (29%)
  blocking collectives  116 us (25%)
  other arithmetic  24 us (5%)
  matrix products  23.5 us (5%)
  starting transfers between devices  9.79 us (2%)
    all_to_all x2, blocking collectives, body(): lax.all_to_all(outbox, 'expert', split_axis=0, concat_axis=0, tiled=True)  116 us
    all_to_all x2, waiting for transfers between devices, body(): lax.all_to_all(served, 'expert', split_axis=0, concat_axis=0, tiled=True)  105 us
    scatter x2, local copies, waits for them, and re-layouts, body(): jnp.zeros((experts, capacity, width), jnp.bfloat16).at[expert_ids, slots]  97.6 us
    ppermute x2, waiting for transfers between devices, from_behind(): return lax.ppermute(value, axis, pairs)  45.7 us
    dot_general x2, matrix products, body(): jnp.dot(hidden, down_proj, preferred_element_type=jnp.float32)  23.5 us
    reduce_sum x2, other arithmetic, body(): jnp.sum(picked * weights_now[..., None], axis=1)  17.5 us
    gather x2, local copies, waits for them, and re-layouts, body(): picked = returned[expert_ids, slots].astype(jnp.float32)  17.1 us
    convert_element_type x2, local copies, waits for them, and re-layouts, body(): picked = returned[expert_ids, slots].astype(jnp.float32)  11.4 us
  transfers between devices with their start and end apart: 4, of which 4 were waited for; matrix products, arithmetic and copies ran while one was open for 1% of the time, Pallas kernels for 0%

commit v1 on v0

--- a/solution.py
+++ b/solution.py
@@ -1,15 +1,222 @@
+import functools
+
 import jax
 import jax.numpy as jnp
 from jax import lax
+from jax.experimental import pallas as pl
+from jax.experimental.pallas import tpu as pltpu
 from jax.sharding import PartitionSpec as P
 
-STOPS = 2
+MESH = pl.DeviceIdType.MESH
+VMEM_ROOM = 56 << 20
 
 
 def from_behind(value, axis, steps):
     count = lax.axis_size(axis)
     pairs = [(source, (source + steps) % count) for source in range(count)]
     return lax.ppermute(value, axis, pairs)
+
+
+def tables(routes, combine, experts, capacity):
+    tok_rows = routes.shape[1]
+    names = jnp.arange(experts, dtype=jnp.int32)
+    chosen = (routes[..., None] == names).astype(jnp.float32)
+    named = jnp.sum(chosen, axis=2)
+    weight = jnp.sum(chosen * combine[..., None], axis=2)
+    earlier = jnp.tril(jnp.ones((tok_rows, tok_rows), jnp.float32), -1)
+    before = jnp.einsum("rq,vqe->vre", earlier, named, preferred_element_type=jnp.float32)
+    slot = jnp.where(named > 0, before, -1.0)
+    places = jnp.arange(capacity, dtype=jnp.float32)
+    turned = jnp.swapaxes(slot, 1, 2)
+    pick = (turned[:, :, None, :] == places[None, None, :, None]).astype(jnp.bfloat16)
+    bring = jnp.where(slot[..., None] == places, weight[..., None], 0.0)
+    high = lax.reduce_precision(bring, 8, 7)
+    low = bring - high
+    stops = routes.shape[0]
+    slots = experts * capacity
+    both = jnp.stack([high, low], axis=1).astype(jnp.bfloat16)
+    return pick.reshape(stops, slots, tok_rows), both.reshape(stops, 2, tok_rows, slots)
+
+
+def relay_kernel(
+    stops, experts, sections, capacity, step,
+    state_ref, pick_ref, bring_ref, gain_ref, up_hbm, down_hbm, out_ref,
+    up_ref, down_ref, later, mixbox, outbox, inbox, servebox, retbox, total, hidden, square,
+    weight_sem, send_out, recv_out, send_ret, recv_ret, send_sec, recv_sec,
+):
+    me = lax.axis_index("expert")
+    here = lax.axis_index("section")
+    ahead, behind = lax.rem(here + 1, sections), lax.rem(here + sections - 1, sections)
+    tok_rows, width = state_ref.shape
+    chunks = width // step
+    slots = experts * capacity
+
+    fetch_up = pltpu.make_async_copy(up_hbm, up_ref, weight_sem.at[0])
+    fetch_down = pltpu.make_async_copy(down_hbm, down_ref, weight_sem.at[1])
+    fetch_up.start()
+    fetch_down.start()
+
+    barrier = pltpu.get_barrier_semaphore()
+    for apart in range(1, experts):
+        peer = lax.rem(me + apart, experts)
+        pl.semaphore_signal(barrier, inc=1, device_id={"expert": peer}, device_id_type=MESH)
+    for peer in (ahead, behind):
+        pl.semaphore_signal(barrier, inc=1, device_id={"section": peer}, device_id_type=MESH)
+    pl.semaphore_wait(barrier, experts + 1)
+
+    def cols(k):
+        return pl.ds(pl.multiple_of(k * step, step), step)
+
+    def over_expert(source, target, send, recv, visit, apart, k):
+        peer = lax.rem(me + apart, experts)
+        return pltpu.make_async_remote_copy(
+            src_ref=source.at[visit, peer, :, cols(k)],
+            dst_ref=target.at[visit, me, :, cols(k)],
+            send_sem=send.at[visit, apart - 1, k],
+            recv_sem=recv.at[visit, apart - 1, k],
+            device_id={"expert": peer},
+            device_id_type=MESH,
+        )
+
+    def dispatch_copy(visit, apart, k):
+        return over_expert(outbox, inbox, send_out, recv_out, visit, apart, k)
+
+    def return_copy(visit, apart, k):
+        return over_expert(servebox, retbox, send_ret, recv_ret, visit, apart, k)
+
+    def section_copy(visit, k):
+        target = out_ref if visit == stops - 1 else later.at[visit]
+        return pltpu.make_async_remote_copy(
+            src_ref=mixbox.at[visit, :, cols(k)],
+            dst_ref=target.at[:, cols(k)],
+            send_sem=send_sec.at[visit, k],
+            recv_sem=recv_sec.at[visit, k],
+            device_id={"section": ahead},
+            device_id_type=MESH,
+        )
+
+    def state_of(visit):
+        return state_ref if visit == 0 else later.at[visit - 1]
+
+    def dispatch(visit, k):
+        block = state_of(visit)[:, cols(k)]
+        rows = jnp.dot(pick_ref[visit], block, preferred_element_type=jnp.float32)
+        rows = rows.reshape(experts, capacity, step).astype(jnp.bfloat16)
+        outbox[visit, :, :, cols(k)] = rows
+        for apart in range(1, experts):
+            dispatch_copy(visit, apart, k).start()
+        inbox[visit, me, :, cols(k)] = outbox[visit, me, :, cols(k)]
+
+    def expand(visit, k):
+        for apart in range(1, experts):
+            dispatch_copy(visit, apart, k).wait_recv()
+        rows = inbox[visit, :, :, cols(k)].astype(jnp.float32).reshape(slots, step)
+        square[...] += jnp.sum(rows * rows, axis=1, keepdims=True)
+        scaled = (rows * gain_ref[:, cols(k)]).astype(jnp.bfloat16)
+        total[...] += jnp.dot(scaled, up_ref[cols(k), :], preferred_element_type=jnp.float32)
+
+    def serve(visit, k):
+        rows = jnp.dot(hidden[...], down_ref[:, cols(k)], preferred_element_type=jnp.float32)
+        rows = rows.reshape(experts, capacity, step).astype(jnp.bfloat16)
+        servebox[visit, :, :, cols(k)] = rows
+        for apart in range(1, experts):
+            return_copy(visit, apart, k).start()
+        retbox[visit, me, :, cols(k)] = servebox[visit, me, :, cols(k)]
+
+    def mix(visit, k):
+        for apart in range(1, experts):
+            return_copy(visit, apart, k).wait_recv()
+        rows = retbox[visit, :, :, cols(k)].astype(jnp.float32).reshape(slots, step)
+        rows = rows.astype(jnp.bfloat16)
+        added = jnp.dot(bring_ref[visit, 0], rows, preferred_element_type=jnp.float32)
+        added += jnp.dot(bring_ref[visit, 1], rows, preferred_element_type=jnp.float32)
+        wide = state_of(visit)[:, cols(k)].astype(jnp.float32)
+        mixbox[visit, :, cols(k)] = (wide + added).astype(jnp.bfloat16)
+        section_copy(visit, k).start()
+
+    def each(first, work):
+        def turn(k, carry):
+            work(k)
+            return carry
+
+        lax.fori_loop(first, chunks, turn, 0)
+
+    each(0, lambda k: dispatch(0, k))
+    fetch_up.wait()
+    for visit in range(stops):
+        total[...] = jnp.zeros_like(total)
+        square[...] = jnp.zeros_like(square)
+        each(0, lambda k: expand(visit, k))
+        factor = lax.rsqrt(square[...] * (1.0 / width) + 1e-06)
+        before = total[...] * factor
+        hidden[...] = (before * jax.nn.sigmoid(before)).astype(jnp.bfloat16)
+        if visit == 0:
+            fetch_down.wait()
+        each(0, lambda k: serve(visit, k))
+        if visit < stops - 1:
+            mix(visit, 0)
+
+            def both(k):
+                mix(visit, k)
+                section_copy(visit, k - 1).wait_recv()
+                dispatch(visit + 1, k - 1)
+
+            each(1, both)
+            section_copy(visit, chunks - 1).wait_recv()
+            dispatch(visit + 1, chunks - 1)
+        else:
+            each(0, lambda k: mix(visit, k))
+            each(0, lambda k: section_copy(visit, k).wait_recv())
+
+    for visit in range(stops):
+
+        def drain(k):
+            for apart in range(1, experts):
+                dispatch_copy(visit, apart, k).wait_send()
+                return_copy(visit, apart, k).wait_send()
+            section_copy(visit, k).wait_send()
+
+        each(0, drain)
+
+
+def kernel_body(activations, routes, combine, norm_gain, up_weight, down_weight):
+    state = activations[0]
+    experts, sections = lax.axis_size("expert"), lax.axis_size("section")
+    tok_rows, width = state.shape
+    stops, chosen = routes.shape[0], routes.shape[3]
+    inner = up_weight.shape[3]
+    capacity = tok_rows * chosen // experts * 9 // 8
+    slots = experts * capacity
+    step = 512 if width % 512 == 0 else width
+    chunks = width // step
+    pick, bring = tables(routes[:, 0], combine[:, 0], experts, capacity)
+    vmem = pl.BlockSpec(memory_space=pltpu.VMEM)
+    anywhere = pl.BlockSpec(memory_space=pl.ANY)
+    box = pltpu.VMEM((stops, experts, capacity, width), jnp.bfloat16)
+    pair = pltpu.SemaphoreType.DMA((stops, experts - 1, chunks))
+    line = pltpu.SemaphoreType.DMA((stops, chunks))
+    out = pl.pallas_call(
+        functools.partial(relay_kernel, stops, experts, sections, capacity, step),
+        out_shape=jax.ShapeDtypeStruct((tok_rows, width), jnp.bfloat16),
+        in_specs=[vmem] * 4 + [anywhere] * 2,
+        out_specs=anywhere,
+        scratch_shapes=[
+            pltpu.VMEM((width, inner), jnp.bfloat16),
+            pltpu.VMEM((inner, width), jnp.bfloat16),
+            pltpu.VMEM((max(stops - 1, 1), tok_rows, width), jnp.bfloat16),
+            pltpu.VMEM((stops, tok_rows, width), jnp.bfloat16),
+            box, box, box, box,
+            pltpu.VMEM((slots, inner), jnp.float32),
+            pltpu.VMEM((slots, inner), jnp.bfloat16),
+            pltpu.VMEM((slots, 1), jnp.float32),
+            pltpu.SemaphoreType.DMA((2,)),
+            pair, pair, pair, pair, line, line,
+        ],
+        compiler_params=pltpu.CompilerParams(
+            collective_id=0, has_side_effects=True, vmem_limit_bytes=60 << 20
+        ),
+    )(state, pick, bring, norm_gain, up_weight[0, 0], down_weight[0, 0])
+    return out[None]
 
 
 def slot_of(expert_ids, experts):
@@ -19,7 +226,7 @@
     return jnp.sum(before * onehot, axis=1).reshape(expert_ids.shape)
 
 
-def body(activations, routes, combine, norm_gain, up_weight, down_weight):
+def plain_body(activations, routes, combine, norm_gain, up_weight, down_weight):
     state = activations[0]
     gain_row = norm_gain[0]
     up_proj = up_weight[0, 0]
@@ -29,7 +236,7 @@
     width = state.shape[1]
     chosen = routes.shape[3]
     capacity = tok_rows * chosen // experts * 9 // 8
-    for visit in range(STOPS):
+    for visit in range(routes.shape[0]):
         expert_ids = routes[visit, 0]
         weights_now = combine[visit, 0]
         wide_state = state.astype(jnp.float32)
@@ -57,6 +264,17 @@
         mixed = (wide_state + jnp.sum(picked * weights_now[..., None], axis=1)).astype(jnp.bfloat16)
         state = from_behind(mixed, "section", 1)
     return state[None]
+
+
+def body(activations, routes, combine, norm_gain, up_weight, down_weight):
+    experts = lax.axis_size("expert")
+    tok_rows, width = activations.shape[1:]
+    stops, inner = routes.shape[0], up_weight.shape[3]
+    capacity = tok_rows * routes.shape[3] // experts * 9 // 8
+    boxes = 4 * stops * experts * capacity * width * 2
+    rest = 4 * width * inner + (2 * stops + 1) * tok_rows * width * 2 + experts * capacity * inner * 6
+    run = kernel_body if boxes + rest <= VMEM_ROOM else plain_body
+    return run(activations, routes, combine, norm_gain, up_weight, down_weight)
 
 
 def solution(mesh):

time: 472 us -> 228 us (0.48); the launches traced: 464 us -> 228 us
  Pallas kernels: 0 us -> 223 us
  waiting for transfers between devices: 151 us -> 0 us
  local copies, waits for them, and re-layouts: 139 us -> 2.75 us
  blocking collectives: 116 us -> 0 us
  matrix products: 23.5 us -> 0.2 us
  other arithmetic: 24 us -> 2.41 us
  starting transfers between devices: 9.79 us -> 0 us
    pallas_call x0 -> x1, Pallas kernels: none -> 223 us  [kernel_body(): pl.pallas_call(functools.partial(relay_kernel, stops, experts, sections,...]
    all_to_all x2 -> x0, blocking collectives: 116 us -> none  [body(): lax.all_to_all(outbox, 'expert', split_axis=0, concat_axis=0, tiled=True)]
    all_to_all x2 -> x0, waiting for transfers between devices: 105 us -> none  [body(): lax.all_to_all(served, 'expert', split_axis=0, concat_axis=0, tiled=True)]
    scatter x2 -> x0, local copies, waits for them, and re-layouts: 97.6 us -> none  [body(): jnp.zeros((experts, capacity, width), jnp.bfloat16).at[expert_ids, slots]]
    ppermute x2 -> x0, waiting for transfers between devices: 45.7 us -> none  [from_behind(): return lax.ppermute(value, axis, pairs)]
    dot_general x2 -> x1, matrix products: 23.5 us -> 0.2 us  [tables(): jnp.einsum('rq,vqe->vre', earlier, named, preferred_element_type=jnp.floa...]
    reduce_sum x6 -> x1, other arithmetic: 19.4 us -> 0.71 us  [tables(): weight = jnp.sum(chosen * combine[..., None], axis=2)]
    gather x2 -> x0, local copies, waits for them, and re-layouts: 17.1 us -> none  [body(): picked = returned[expert_ids, slots].astype(jnp.float32)]
  transfers between devices with their start and end apart: 4 -> 0, of which waited for: 4 -> 0; matrix products, arithmetic and copies ran while one was open for 1% -> 0% of each run, Pallas kernels for 0% -> 0%
where the time goes in v1:
time: 228 us
  Pallas kernels  223 us (98%)
  local copies, waits for them, and re-layouts  2.75 us (1%)
  other arithmetic  2.41 us (1%)
    pallas_call x1, Pallas kernels, kernel_body(): pl.pallas_call(functools.partial(relay_kernel, stops, experts, sections,...  223 us

profile of v1, /device:TPU:0, one launch (start us, length us, event | category | flops | bytes accessed | tf_op | source)
XLA Modules:
  0.0 228.0 jit_solution(2227670115324363696)
XLA Ops:
  0.0 0.1 eq.74
  0.1 0.7 select_reduce_fusion
  0.8 0.2 bitcast_select_fusion
  1.0 0.8 fusion.1.pick_ref
  1.8 0.2 copy.14
  2.0 0.2 copy.15
  2.2 0.1 reduce-precision_convert_fusion
  2.3 0.8 pad_maximum_fusion.bring_ref
  3.1 222.6 %shard_map.64 = bf16[128,4096]{1,0:T(8,128)(2,1)} custom-call(bf16[128,4096]{1,0:T(8,128)(2,1)} %bitcast.27, bf16[2,288,128]{2,1,0:T(8,128)(2,1)} %fusion.1.pick_ref, bf16[2,2,128,288]{3,2,1,0:T(8,128)(2,1)} %pad_maximum_fusion.bring_ref, f32[1,4096]{1,0:T(1,128)} %gain_ref.1, bf16[4096,768]{1,0:T(8,128)(2,1)} %bitcast.22, bf16[768,4096]{1,0:T(8,128)(2,1)} %bitcast.23), custom_call_target="tpu_custom_call" | custom-call | tf_op jit(solution)/shard_map/pallas_call | solution.py:198
  225.7 2.3 %copy.17 = bf16[1,128,4096]{2,1,0:T(8,128)(2,1)} copy(bf16[1,128,4096]{2,1,0:T(8,128)(2,1)} %bitcast.24) | data formatting | bytes 2097152
  (5 shorter events, 0.1 us)

commit v2 on v0

--- a/solution.py
+++ b/solution.py
@@ -1,15 +1,409 @@
+import functools
+
 import jax
 import jax.numpy as jnp
 from jax import lax
+from jax.experimental import pallas as pl
+from jax.experimental.pallas import tpu as pltpu
 from jax.sharding import PartitionSpec as P
 
-STOPS = 2
+MESH = pl.DeviceIdType.MESH
+VMEM_ROOM = 56 << 20
 
 
 def from_behind(value, axis, steps):
     count = lax.axis_size(axis)
     pairs = [(source, (source + steps) % count) for source in range(count)]
     return lax.ppermute(value, axis, pairs)
+
+
+def tables(routes, combine, experts, capacity):
+    stops, tok_rows = routes.shape[:2]
+    names = jnp.arange(experts, dtype=jnp.int32)
+    chosen = (routes[..., None] == names).astype(jnp.float32)
+    named = jnp.sum(chosen, axis=2)
+    weight = jnp.sum(chosen * combine[..., None], axis=2)
+    earlier = jnp.tril(jnp.ones((tok_rows, tok_rows), jnp.float32), -1)
+    before = jnp.einsum("rq,vqe->vre", earlier, named, preferred_element_type=jnp.float32)
+    slot = jnp.where(named > 0, before, -1.0)
+    places = jnp.arange(capacity, dtype=jnp.float32)
+    turned = jnp.swapaxes(slot, 1, 2)
+    turned_weight = jnp.swapaxes(weight, 1, 2)
+    pick = (turned[:, :, None, :] == places[None, None, :, None]).astype(jnp.bfloat16)
+    half = experts // 2
+    bring = jnp.where(slot[..., None] == places, weight[..., None], 0.0)
+    bring = jnp.swapaxes(bring.reshape(stops, tok_rows, 2, half * capacity), 1, 2)
+    high = lax.reduce_precision(bring, 8, 7)
+    low = bring - high
+    both = jnp.stack([high, low], axis=2).astype(jnp.bfloat16)
+    tab = jnp.concatenate(
+        [
+            turned.reshape(stops, 2, half, tok_rows),
+            turned_weight.reshape(stops, 2, half, tok_rows),
+            jnp.zeros((stops, 2, 8 - 2 * half, tok_rows), jnp.float32),
+        ],
+        axis=2,
+    )
+    return pick.reshape(stops, 2, half * capacity, tok_rows), both, jnp.swapaxes(tab, 0, 1)
+
+
+def relay_kernel(
+    stops, sections, capacity, step, edge, lead, lag,
+    state_ref, pick_ref, bring_ref, tab_ref, gain_ref, up_hbm, down_hbm, out_ref,
+    up_ref, down_ref, later, mixbox, outbox, inbox, servebox, retbox,
+    crossbox, pickbox, gatherbox, partbox, partin, tabbox, far_pick, far_bring,
+    total, hidden, square, weight_sem,
+    send_out, recv_out, send_ret, recv_ret, send_sec, recv_sec,
+    send_cross, recv_cross, send_fwd, send_gather, recv_gather, send_part, recv_part,
+    send_tab, recv_tab,
+):
+    me = lax.axis_index("expert")
+    here = lax.axis_index("section")
+    ahead, behind = lax.rem(here + 1, sections), lax.rem(here + sections - 1, sections)
+    half, mine = me // 2, lax.rem(me, 2)
+    partner = 2 * half + 1 - mine
+    other = 2 * (1 - half)
+    gate = 2 - half
+    inner = me == 1 + half
+    outer = me == 3 * half
+    tok_rows, width = state_ref.shape
+    chunks = width // step
+    near = 2 * capacity
+    last = chunks - edge
+
+    fetch_up = pltpu.make_async_copy(up_hbm, up_ref, weight_sem.at[0])
+    fetch_down = pltpu.make_async_copy(down_hbm, down_ref, weight_sem.at[1])
+    fetch_up.start()
+    fetch_down.start()
+
+    barrier = pltpu.get_barrier_semaphore()
+    for apart in range(1, 4):
+        peer = lax.rem(me + apart, 4)
+        pl.semaphore_signal(barrier, inc=1, device_id={"expert": peer}, device_id_type=MESH)
+    for peer in (ahead, behind):
+        pl.semaphore_signal(barrier, inc=1, device_id={"section": peer}, device_id_type=MESH)
+    pl.semaphore_wait(barrier, 5)
+
+    def cols(k):
+        return pl.ds(pl.multiple_of(k * step, step), step)
+
+    def send(source, target, send_sem, recv_sem, peer):
+        return pltpu.make_async_remote_copy(
+            src_ref=source, dst_ref=target, send_sem=send_sem, recv_sem=recv_sem,
+            device_id={"expert": peer}, device_id_type=MESH,
+        )
+
+    def when(condition):
+        return pl.when(condition)
+
+    def tab_copy(place):
+        return send(tab_ref.at[1 - half], tabbox.at[place], send_tab, recv_tab.at[place], gate)
+
+    def out_copy(v, k, peer, block):
+        return send(outbox.at[v, peer, :, cols(k)], inbox.at[v, block, :, cols(k)],
+                    send_out.at[v, peer, k], recv_out.at[v, block, k], peer)
+
+    def cross_copy(v, k, place):
+        return send(state_of(v).at[:, cols(k)], crossbox.at[v, place, :, cols(k)],
+                    send_cross.at[v, k], recv_cross.at[v, place, k], gate)
+
+    def forward_copy(v, k, q):
+        return send(pickbox.at[v, q, 1 - mine, :, cols(k)], inbox.at[v, other + q, :, cols(k)],
+                    send_fwd.at[v, q, k], recv_out.at[v, other + q, k], partner)
+
+    def ret_copy(v, k, peer, expert):
+        return send(servebox.at[v, peer, :, cols(k)], retbox.at[v, expert, :, cols(k)],
+                    send_ret.at[v, peer, k], recv_ret.at[v, expert, k], peer)
+
+    def gather_copy(v, k, q, place):
+        return send(servebox.at[v, other + q, :, cols(k)], gatherbox.at[v, q, place, :, cols(k)],
+                    send_gather.at[v, q, k], recv_gather.at[v, q, k], partner)
+
+    def part_copy(v, k, q):
+        return send(partbox.at[v, q, :, cols(k)], partin.at[v, :, cols(k)],
+                    send_part.at[v, q, k], recv_part.at[v, k], other + q)
+
+    def section_copy(v, k):
+        target = out_ref if v == stops - 1 else later.at[v]
+        return pltpu.make_async_remote_copy(
+            src_ref=mixbox.at[v, :, cols(k)], dst_ref=target.at[:, cols(k)],
+            send_sem=send_sec.at[v, k], recv_sem=recv_sec.at[v, k],
+            device_id={"section": ahead}, device_id_type=MESH,
+        )
+
+    def state_of(v):
+        return state_ref if v == 0 else later.at[v - 1]
+
+    def dispatch(v, k):
+        @when(k < last)
+        def _():
+            cross_copy(v, k, mine).start()
+
+        block = state_of(v)[:, cols(k)]
+        rows = jnp.dot(pick_ref[v, half], block, preferred_element_type=jnp.float32)
+        outbox[v, pl.ds(2 * half, 2), :, cols(k)] = rows.reshape(2, capacity, step).astype(jnp.bfloat16)
+
+        @when(k >= last)
+        def _():
+            far = jnp.dot(pick_ref[v, 1 - half], block, preferred_element_type=jnp.float32)
+            outbox[v, pl.ds(other, 2), :, cols(k)] = far.reshape(2, capacity, step).astype(jnp.bfloat16)
+            for q in range(2):
+                out_copy(v, k, other + q, me).start()
+
+        out_copy(v, k, partner, me).start()
+        inbox[v, me, :, cols(k)] = outbox[v, me, :, cols(k)]
+
+    def pass_on(v, k):
+        @when(inner)
+        def _():
+            for q in range(2):
+                cross_copy(v, k, q).wait_recv()
+                rows = jnp.dot(far_pick[v, q], crossbox[v, q, :, cols(k)], preferred_element_type=jnp.float32)
+                pickbox[v, q, :, :, cols(k)] = rows.reshape(2, capacity, step).astype(jnp.bfloat16)
+                forward_copy(v, k, q).start()
+                inbox[v, other + q, :, cols(k)] = pickbox[v, q, mine, :, cols(k)]
+
+    def expand(v, k):
+        out_copy(v, k, partner, partner).wait_recv()
+
+        @when(jnp.logical_or(outer, k >= last))
+        def _():
+            for q in range(2):
+                out_copy(v, k, partner, other + q).wait_recv()
+
+        rows = inbox[v, :, :, cols(k)].astype(jnp.float32).reshape(2 * near, step)
+        square[...] += jnp.sum(rows * rows, axis=1, keepdims=True)
+        scaled = (rows * gain_ref[:, cols(k)]).astype(jnp.bfloat16)
+        total[...] += jnp.dot(scaled, up_ref[cols(k), :], preferred_element_type=jnp.float32)
+
+    def serve(v, k):
+        rows = jnp.dot(hidden[...], down_ref[:, cols(k)], preferred_element_type=jnp.float32)
+        servebox[v, :, :, cols(k)] = rows.reshape(4, capacity, step).astype(jnp.bfloat16)
+
+        @when(k < edge)
+        def _():
+            for q in range(2):
+                ret_copy(v, k, other + q, me).start()
+
+        @when(jnp.logical_and(outer, k >= edge))
+        def _():
+            for q in range(2):
+                gather_copy(v, k, q, mine).start()
+
+        ret_copy(v, k, partner, me).start()
+
+        @when(jnp.logical_and(inner, k >= edge))
+        def _():
+            for q in range(2):
+                gatherbox[v, q, mine, :, cols(k)] = servebox[v, other + q, :, cols(k)]
+
+        retbox[v, me, :, cols(k)] = servebox[v, me, :, cols(k)]
+
+    def narrow(rows):
+        return rows.astype(jnp.float32).reshape(near, step).astype(jnp.bfloat16)
+
+    def combine(v, k):
+        @when(inner)
+        def _():
+            for q in range(2):
+                gather_copy(v, k, q, 1 - mine).wait_recv()
+                rows = narrow(gatherbox[v, q, :, :, cols(k)])
+                part = jnp.dot(far_bring[v, q, 0], rows, preferred_element_type=jnp.float32)
+                part += jnp.dot(far_bring[v, q, 1], rows, preferred_element_type=jnp.float32)
+                partbox[v, q, :, cols(k)] = part.astype(jnp.bfloat16)
+                part_copy(v, k, q).start()
+
+    def mix(v, k):
+        ret_copy(v, k, partner, partner).wait_recv()
+        rows = narrow(retbox[v, pl.ds(2 * half, 2), :, cols(k)])
+        added = jnp.dot(bring_ref[v, half, 0], rows, preferred_element_type=jnp.float32)
+        added += jnp.dot(bring_ref[v, half, 1], rows, preferred_element_type=jnp.float32)
+        wide = state_of(v)[:, cols(k)].astype(jnp.float32) + added
+
+        @when(k < edge)
+        def _():
+            for q in range(2):
+                ret_copy(v, k, partner, other + q).wait_recv()
+            far = narrow(retbox[v, pl.ds(other, 2), :, cols(k)])
+            more = jnp.dot(bring_ref[v, 1 - half, 0], far, preferred_element_type=jnp.float32)
+            more += jnp.dot(bring_ref[v, 1 - half, 1], far, preferred_element_type=jnp.float32)
+            mixbox[v, :, cols(k)] = (wide + more).astype(jnp.bfloat16)
+
+        @when(k >= edge)
+        def _():
+            part_copy(v, k, 0).wait_recv()
+            more = partin[v, :, cols(k)].astype(jnp.float32)
+            mixbox[v, :, cols(k)] = (wide + more).astype(jnp.bfloat16)
+
+        section_copy(v, k).start()
+
+    def far_tables(q):
+        tab_copy(q).wait_recv()
+        for v in range(stops):
+            tab = tabbox[q, v]
+            place = lax.broadcasted_iota(jnp.int32, (capacity, tok_rows), 0).astype(jnp.float32)
+            chosen = [tab[j : j + 1] == place for j in range(2)]
+            picks = [jnp.where(c, 1.0, 0.0) for c in chosen]
+            far_pick[v, q] = jnp.concatenate(picks, axis=0).astype(jnp.bfloat16)
+            brings = [jnp.where(c, tab[2 + j : 3 + j], 0.0) for j, c in enumerate(chosen)]
+            brings.append(jnp.zeros((-near % tok_rows, tok_rows), jnp.float32))
+            turned = jnp.concatenate(brings, axis=0).T[:, :near]
+            high = turned.astype(jnp.bfloat16)
+            far_bring[v, q, 0] = high
+            far_bring[v, q, 1] = (turned - high.astype(jnp.float32)).astype(jnp.bfloat16)
+
+    def each(first, end, work):
+        def turn(k, carry):
+            work(k)
+            return carry
+
+        lax.fori_loop(first, end, turn, 0)
+
+    tab_copy(mine).start()
+    each(0, chunks, lambda k: dispatch(0, k))
+
+    @when(inner)
+    def _():
+        for q in range(2):
+            far_tables(q)
+
+    fetch_up.wait()
+    passed = 0
+    for v in range(stops):
+        total[...] = jnp.zeros_like(total)
+        square[...] = jnp.zeros_like(square)
+
+        def take(k):
+            @when(jnp.logical_and(k >= passed, k < last))
+            def _():
+                pass_on(v, k)
+
+            expand(v, k)
+
+        each(0, chunks, take)
+        factor = lax.rsqrt(square[...] * (1.0 / width) + 1e-06)
+        before = total[...] * factor
+        hidden[...] = (before * jax.nn.sigmoid(before)).astype(jnp.bfloat16)
+        if v == 0:
+            fetch_down.wait()
+        each(0, chunks, lambda k: serve(v, k))
+        each(edge, max(edge, lead), lambda k: combine(v, k))
+
+        def turn(k):
+            @when(jnp.logical_and(k + lead >= edge, k + lead < chunks))
+            def _():
+                combine(v, k + lead)
+
+            mix(v, k)
+            if v < stops - 1:
+
+                @when(k >= 1)
+                def _():
+                    section_copy(v, k - 1).wait_recv()
+                    dispatch(v + 1, k - 1)
+
+                @when(jnp.logical_and(k >= lag, k - lag < last))
+                def _():
+                    pass_on(v + 1, k - lag)
+
+        each(0, chunks, turn)
+        if v < stops - 1:
+            section_copy(v, chunks - 1).wait_recv()
+            dispatch(v + 1, chunks - 1)
+            passed = min(chunks - lag, last)
+        else:
+            each(0, chunks, lambda k: section_copy(v, k).wait_recv())
+
+    for v in range(stops):
+
+        def drain(k):
+            out_copy(v, k, partner, me).wait_send()
+            ret_copy(v, k, partner, me).wait_send()
+            section_copy(v, k).wait_send()
+
+            @when(k < last)
+            def _():
+                cross_copy(v, k, mine).wait_send()
+
+            @when(jnp.logical_and(inner, k < last))
+            def _():
+                for q in range(2):
+                    forward_copy(v, k, q).wait_send()
+
+            @when(jnp.logical_and(inner, k >= edge))
+            def _():
+                for q in range(2):
+                    part_copy(v, k, q).wait_send()
+
+            @when(jnp.logical_and(outer, k >= edge))
+            def _():
+                for q in range(2):
+                    gather_copy(v, k, q, mine).wait_send()
+
+            @when(k >= last)
+            def _():
+                for q in range(2):
+                    out_copy(v, k, other + q, me).wait_send()
+
+            @when(k < edge)
+            def _():
+                for q in range(2):
+                    ret_copy(v, k, other + q, me).wait_send()
+
+        each(0, chunks, drain)
+    tab_copy(mine).wait_send()
+
+
+def kernel_body(activations, routes, combine, norm_gain, up_weight, down_weight):
+    state = activations[0]
+    experts, sections = lax.axis_size("expert"), lax.axis_size("section")
+    tok_rows, width = state.shape
+    stops, chosen = routes.shape[0], routes.shape[3]
+    inner = up_weight.shape[3]
+    capacity = tok_rows * chosen // experts * 9 // 8
+    slots, near = experts * capacity, experts // 2 * capacity
+    step = 256 if width % 256 == 0 else width
+    chunks = width // step
+    pick, bring, tab = tables(routes[:, 0], combine[:, 0], experts, capacity)
+    vmem = pl.BlockSpec(memory_space=pltpu.VMEM)
+    anywhere = pl.BlockSpec(memory_space=pl.ANY)
+    dma = pltpu.SemaphoreType.DMA
+    half_rows = (stops, experts // 2, experts // 2, capacity, width)
+    box = pltpu.VMEM((stops, experts, capacity, width), jnp.bfloat16)
+    whole = pltpu.VMEM((stops, tok_rows, width), jnp.bfloat16)
+    twice = pltpu.VMEM((stops, experts // 2, tok_rows, width), jnp.bfloat16)
+    by_expert, by_half, line = dma((stops, experts, chunks)), dma((stops, 2, chunks)), dma((stops, chunks))
+    out = pl.pallas_call(
+        functools.partial(relay_kernel, stops, sections, capacity, step, 2, 3, 3),
+        out_shape=jax.ShapeDtypeStruct((tok_rows, width), jnp.bfloat16),
+        in_specs=[vmem] * 5 + [anywhere] * 2,
+        out_specs=anywhere,
+        scratch_shapes=[
+            pltpu.VMEM((width, inner), jnp.bfloat16),
+            pltpu.VMEM((inner, width), jnp.bfloat16),
+            pltpu.VMEM((max(stops - 1, 1), tok_rows, width), jnp.bfloat16),
+            whole,
+            box, box, box, box,
+            twice,
+            pltpu.VMEM(half_rows, jnp.bfloat16),
+            pltpu.VMEM(half_rows, jnp.bfloat16),
+            twice, whole,
+            pltpu.VMEM((2, stops, 8, tok_rows), jnp.float32),
+            pltpu.VMEM((stops, 2, near, tok_rows), jnp.bfloat16),
+            pltpu.VMEM((stops, 2, 2, tok_rows, near), jnp.bfloat16),
+            pltpu.VMEM((slots, inner), jnp.float32),
+            pltpu.VMEM((slots, inner), jnp.bfloat16),
+            pltpu.VMEM((slots, 1), jnp.float32),
+            dma((2,)),
+            by_expert, by_expert, by_expert, by_expert, line, line,
+            line, by_half, by_half, by_half, by_half, by_half, line,
+            dma, dma((2,)),
+        ],
+        compiler_params=pltpu.CompilerParams(
+            collective_id=0, has_side_effects=True, vmem_limit_bytes=62 << 20
+        ),
+    )(state, pick, bring, tab, norm_gain, up_weight[0, 0], down_weight[0, 0])
+    return out[None]
 
 
 def slot_of(expert_ids, experts):
@@ -19,7 +413,7 @@
     return jnp.sum(before * onehot, axis=1).reshape(expert_ids.shape)
 
 
-def body(activations, routes, combine, norm_gain, up_weight, down_weight):
+def plain_body(activations, routes, combine, norm_gain, up_weight, down_weight):
     state = activations[0]
     gain_row = norm_gain[0]
     up_proj = up_weight[0, 0]
@@ -29,7 +423,7 @@
     width = state.shape[1]
     chosen = routes.shape[3]
     capacity = tok_rows * chosen // experts * 9 // 8
-    for visit in range(STOPS):
+    for visit in range(routes.shape[0]):
         expert_ids = routes[visit, 0]
         weights_now = combine[visit, 0]
         wide_state = state.astype(jnp.float32)
@@ -59,6 +453,18 @@
     return state[None]
 
 
+def body(activations, routes, combine, norm_gain, up_weight, down_weight):
+    experts = lax.axis_size("expert")
+    tok_rows, width = activations.shape[1:]
+    stops, inner = routes.shape[0], up_weight.shape[3]
+    capacity = tok_rows * routes.shape[3] // experts * 9 // 8
+    boxes = 6 * stops * experts * capacity * width * 2
+    rest = 4 * width * inner + (7 * stops + 1) * tok_rows * width * 2 + experts * capacity * inner * 6
+    fits = experts == 4 and boxes + rest <= VMEM_ROOM
+    run = kernel_body if fits else plain_body
+    return run(activations, routes, combine, norm_gain, up_weight, down_weight)
+
+
 def solution(mesh):
     placed = (
         P("section", ("dp", "expert"), None),

time: 472 us -> 232 us (0.49); the launches traced: 464 us -> 232 us
  Pallas kernels: 0 us -> 225 us
  waiting for transfers between devices: 151 us -> 0 us
  local copies, waits for them, and re-layouts: 139 us -> 2.91 us
  blocking collectives: 116 us -> 0 us
  matrix products: 23.5 us -> 0.2 us
  other arithmetic: 24 us -> 3.15 us
  starting transfers between devices: 9.79 us -> 0 us
    pallas_call x0 -> x1, Pallas kernels: none -> 225 us  [kernel_body(): pl.pallas_call(functools.partial(relay_kernel, stops, sections, capacity,...]
    all_to_all x2 -> x0, blocking collectives: 116 us -> none  [body(): lax.all_to_all(outbox, 'expert', split_axis=0, concat_axis=0, tiled=True)]
    all_to_all x2 -> x0, waiting for transfers between devices: 105 us -> none  [body(): lax.all_to_all(served, 'expert', split_axis=0, concat_axis=0, tiled=True)]
    scatter x2 -> x0, local copies, waits for them, and re-layouts: 97.6 us -> none  [body(): jnp.zeros((experts, capacity, width), jnp.bfloat16).at[expert_ids, slots]]
    ppermute x2 -> x0, waiting for transfers between devices: 45.7 us -> none  [from_behind(): return lax.ppermute(value, axis, pairs)]
    dot_general x2 -> x1, matrix products: 23.5 us -> 0.2 us  [tables(): jnp.einsum('rq,vqe->vre', earlier, named, preferred_element_type=jnp.floa...]
    reduce_sum x6 -> x1, other arithmetic: 19.4 us -> 0.71 us  [tables(): weight = jnp.sum(chosen * combine[..., None], axis=2)]
    gather x2 -> x0, local copies, waits for them, and re-layouts: 17.1 us -> none  [body(): picked = returned[expert_ids, slots].astype(jnp.float32)]
  transfers between devices with their start and end apart: 4 -> 0, of which waited for: 4 -> 0; matrix products, arithmetic and copies ran while one was open for 1% -> 0% of each run, Pallas kernels for 0% -> 0%
where the time goes in v2:
time: 232 us
  Pallas kernels  225 us (97%)
  other arithmetic  3.15 us (1%)
  local copies, waits for them, and re-layouts  2.91 us (1%)
    pallas_call x1, Pallas kernels, kernel_body(): pl.pallas_call(functools.partial(relay_kernel, stops, sections, capacity,...  225 us

profile of v2, /device:TPU:0, one launch (start us, length us, event | category | flops | bytes accessed | tf_op | source)
XLA Modules:
  0.0 231.8 jit_solution(16003674214324974125)
XLA Ops:
  0.0 0.1 pad.2.clone
  0.1 0.1 eq.62
  0.2 0.7 select_reduce_fusion
  0.9 0.2 bitcast_select_fusion
  1.1 0.7 maximum_bitcast_fusion.tab_ref
  1.8 0.2 copy.18
  2.0 0.8 fusion.1.pick_ref
  2.8 0.2 copy.19
  3.0 0.1 fusion.3
  3.1 0.9 pad_maximum_fusion.bring_ref
  4.0 225.5 %shard_map.64 = bf16[128,4096]{1,0:T(8,128)(2,1)} custom-call(bf16[128,4096]{1,0:T(8,128)(2,1)} %bitcast.48, bf16[2,2,144,128]{3,2,1,0:T(8,128)(2,1)} %fusion.1.pick_ref, bf16[2,2,2,128,144]{4,3,2,1,0:T(8,128)(2,1)} %pad_maximum_fusion.bring_ref, f32[2,2,8,128]{3,2,1,0:T(8,128)} %maximum_bitcast_fusion.tab_ref, f32[1,4096]{1,0:T(1,128)} %gain_ref.1, ...), custom_call_target="tpu_custom_call" | custom-call | tf_op jit(solution)/shard_map/pallas_call | solution.py:376
  229.5 2.3 copy.28
  (7 shorter events, 0.1 us)

commit v3 on v2

--- a/solution.py
+++ b/solution.py
@@ -48,7 +48,7 @@
 
 
 def relay_kernel(
-    stops, sections, capacity, step, edge, lead, lag,
+    stops, sections, capacity, step, edge, early, lead, lag,
     state_ref, pick_ref, bring_ref, tab_ref, gain_ref, up_hbm, down_hbm, out_ref,
     up_ref, down_ref, later, mixbox, outbox, inbox, servebox, retbox,
     crossbox, pickbox, gatherbox, partbox, partin, tabbox, far_pick, far_bring,
@@ -286,10 +286,14 @@
         hidden[...] = (before * jax.nn.sigmoid(before)).astype(jnp.bfloat16)
         if v == 0:
             fetch_down.wait()
-        each(0, chunks, lambda k: serve(v, k))
+        each(0, jnp.where(outer, chunks, early), lambda k: serve(v, k))
         each(edge, max(edge, lead), lambda k: combine(v, k))
 
         def turn(k):
+            @when(jnp.logical_and(inner, k + early < chunks))
+            def _():
+                serve(v, k + early)
+
             @when(jnp.logical_and(k + lead >= edge, k + lead < chunks))
             def _():
                 combine(v, k + lead)
@@ -374,7 +378,7 @@
     twice = pltpu.VMEM((stops, experts // 2, tok_rows, width), jnp.bfloat16)
     by_expert, by_half, line = dma((stops, experts, chunks)), dma((stops, 2, chunks)), dma((stops, chunks))
     out = pl.pallas_call(
-        functools.partial(relay_kernel, stops, sections, capacity, step, 2, 3, 3),
+        functools.partial(relay_kernel, stops, sections, capacity, step, 2, 9, 8, 6),
         out_shape=jax.ShapeDtypeStruct((tok_rows, width), jnp.bfloat16),
         in_specs=[vmem] * 5 + [anywhere] * 2,
         out_specs=anywhere,

time: 232 us -> 222 us (0.957)
  Pallas kernels: 225 us -> 215 us
    pallas_call x1, Pallas kernels: 225 us -> 215 us  [kernel_body(): pl.pallas_call(functools.partial(relay_kernel, stops, sections, capacity,...]
where the time goes in v3:
time: 222 us
  Pallas kernels  215 us (97%)
  other arithmetic  3.15 us (1%)
  local copies, waits for them, and re-layouts  2.91 us (1%)
    pallas_call x1, Pallas kernels, kernel_body(): pl.pallas_call(functools.partial(relay_kernel, stops, sections, capacity,...  215 us

profile of v3, /device:TPU:0, one launch (start us, length us, event | category | flops | bytes accessed | tf_op | source)
XLA Modules:
  0.0 221.6 jit_solution(14418934413514621398)
XLA Ops:
  0.0 0.1 pad.2.clone
  0.1 0.1 eq.62
  0.2 0.7 select_reduce_fusion
  0.9 0.2 bitcast_select_fusion
  1.1 0.7 maximum_bitcast_fusion.tab_ref
  1.8 0.2 copy.18
  2.0 0.8 fusion.1.pick_ref
  2.8 0.2 copy.19
  3.0 0.1 fusion.3
  3.1 0.9 pad_maximum_fusion.bring_ref
  4.0 215.3 %shard_map.64 = bf16[128,4096]{1,0:T(8,128)(2,1)} custom-call(bf16[128,4096]{1,0:T(8,128)(2,1)} %bitcast.48, bf16[2,2,144,128]{3,2,1,0:T(8,128)(2,1)} %fusion.1.pick_ref, bf16[2,2,2,128,144]{4,3,2,1,0:T(8,128)(2,1)} %pad_maximum_fusion.bring_ref, f32[2,2,8,128]{3,2,1,0:T(8,128)} %maximum_bitcast_fusion.tab_ref, f32[1,4096]{1,0:T(1,128)} %gain_ref.1, ...), custom_call_target="tpu_custom_call" | custom-call | tf_op jit(solution)/shard_map/pallas_call | solution.py:380
  219.3 2.3 %copy.28 = bf16[1,128,4096]{2,1,0:T(8,128)(2,1)} copy(bf16[1,128,4096]{2,1,0:T(8,128)(2,1)} %bitcast.44) | data formatting | bytes 2097152
  (7 shorter events, 0.1 us)

commit v4 on v3

--- a/solution.py
+++ b/solution.py
@@ -366,7 +366,7 @@
     inner = up_weight.shape[3]
     capacity = tok_rows * chosen // experts * 9 // 8
     slots, near = experts * capacity, experts // 2 * capacity
-    step = 256 if width % 256 == 0 else width
+    step = 512 if width % 512 == 0 else width
     chunks = width // step
     pick, bring, tab = tables(routes[:, 0], combine[:, 0], experts, capacity)
     vmem = pl.BlockSpec(memory_space=pltpu.VMEM)
@@ -378,7 +378,7 @@
     twice = pltpu.VMEM((stops, experts // 2, tok_rows, width), jnp.bfloat16)
     by_expert, by_half, line = dma((stops, experts, chunks)), dma((stops, 2, chunks)), dma((stops, chunks))
     out = pl.pallas_call(
-        functools.partial(relay_kernel, stops, sections, capacity, step, 2, 9, 8, 6),
+        functools.partial(relay_kernel, stops, sections, capacity, step, 2, 4, 2, 2),
         out_shape=jax.ShapeDtypeStruct((tok_rows, width), jnp.bfloat16),
         in_specs=[vmem] * 5 + [anywhere] * 2,
         out_specs=anywhere,

time: 222 us -> 217 us (0.977)
  Pallas kernels: 215 us -> 210 us
    pallas_call x1, Pallas kernels: 215 us -> 210 us  [kernel_body(): pl.pallas_call(functools.partial(relay_kernel, stops, sections, capacity,...]
where the time goes in v4:
time: 217 us
  Pallas kernels  210 us (97%)
  other arithmetic  3.15 us (1%)
  local copies, waits for them, and re-layouts  2.91 us (1%)
    pallas_call x1, Pallas kernels, kernel_body(): pl.pallas_call(functools.partial(relay_kernel, stops, sections, capacity,...  210 us

profile of v4, /device:TPU:0, one launch (start us, length us, event | category | flops | bytes accessed | tf_op | source)
XLA Modules:
  0.0 216.6 jit_solution(4729632463653775753)
XLA Ops:
  0.0 0.1 pad.2.clone
  0.1 0.1 eq.62
  0.2 0.7 select_reduce_fusion
  0.9 0.2 bitcast_select_fusion
  1.1 0.7 maximum_bitcast_fusion.tab_ref
  1.8 0.2 copy.18
  2.0 0.8 fusion.1.pick_ref
  2.8 0.2 copy.19
  3.0 0.1 fusion.3
  3.1 0.9 pad_maximum_fusion.bring_ref
  4.0 210.3 %shard_map.64 = bf16[128,4096]{1,0:T(8,128)(2,1)} custom-call(bf16[128,4096]{1,0:T(8,128)(2,1)} %bitcast.48, bf16[2,2,144,128]{3,2,1,0:T(8,128)(2,1)} %fusion.1.pick_ref, bf16[2,2,2,128,144]{4,3,2,1,0:T(8,128)(2,1)} %pad_maximum_fusion.bring_ref, f32[2,2,8,128]{3,2,1,0:T(8,128)} %maximum_bitcast_fusion.tab_ref, f32[1,4096]{1,0:T(1,128)} %gain_ref.1, ...), custom_call_target="tpu_custom_call" | custom-call | tf_op jit(solution)/shard_map/pallas_call | solution.py:380
  214.4 2.3 %copy.28 = bf16[1,128,4096]{2,1,0:T(8,128)(2,1)} copy(bf16[1,128,4096]{2,1,0:T(8,128)(2,1)} %bitcast.44) | data formatting | bytes 2097152
  (7 shorter events, 0.1 us)
